TPU v7x, 32 devices: a whole 2x2x4 slice. The times are simulated.
32 devices in a mesh: grp: 2 (over y), dev: 16 (over z, x, core).
Axes of the slice: x: 2, y: 2, z: 4, core: 2. Of those that a mesh axis runs over, the one named last changes fastest.
Arguments:
- spectra: float32 [256, 2, 2, 4096], P(('grp', 'dev')), may hold values from -100 to 100
- source_pick: int32 [32], P(('grp', 'dev')), may hold values from 0 to 7
- pair_remote: int32 [2, 16, 2, 2], P('grp', 'dev'), may hold values from 0 to 7
- pair_local: int32 [2, 16, 2, 2], P('grp', 'dev'), may hold values from 0 to 7
- pair_count: int32 [2, 16, 2], P('grp', 'dev'), may hold values from 0 to 2, as said below
Outputs:
- group_corr: float32 [256, 16, 512], P(('grp', 'dev'))
- cross_corr: float32 [2, 16, 2, 2, 512], P('grp', 'dev')
Inputs may be any that keep to these rules, and one draw needn't show every extreme that they name: `pair_count`: A block has no pairs with its own group and at most 2 with any other; in every group some block has exactly 2 with some other group.
All inputs are finite; a program needn't handle non-finite values.
Results may differ from a plain program's by a relative error of at most 0.0075.
Values may be sent and summed in bfloat16 or wider, within the bound.
A program may use at most 64 MiB of HBM per device.

v0:
```python
import math
import jax
import jax.numpy as jnp
from jax import lax
from jax.sharding import PartitionSpec as P

F = 4096
LAGS = 512
LAG_BLK = 128
BAND = 64
source_block = 16


def whiten(spectra):
    magnitude = jnp.sqrt(spectra[:, :, 0] * spectra[:, :, 0] + spectra[:, :, 1] * spectra[:, :, 1])
    rows_here, segments, bins = magnitude.shape
    band_mean = jnp.mean(magnitude.reshape(rows_here, segments, bins // BAND, BAND), axis=3) + 1e-05
    divisor = jnp.repeat(band_mean, BAND, axis=2)
    return (spectra / divisor[:, :, None, :]).astype(jnp.bfloat16)


def lag_tables():
    frequency = jnp.arange(F, dtype=jnp.int32)
    lag_index = jnp.arange(LAG_BLK, dtype=jnp.int32)
    phase_index = frequency[:, None] * lag_index[None, :] % (2 * F)
    angles = phase_index.astype(jnp.float32) * (math.pi / F)
    return (jnp.cos(angles).astype(jnp.bfloat16), (-jnp.sin(angles)).astype(jnp.bfloat16))


def lag_turn(block_index):
    frequency = jnp.arange(F, dtype=jnp.int32)
    phase_index = frequency * (LAG_BLK * block_index - LAGS // 2) % (2 * F)
    angles = phase_index.astype(jnp.float32) * (math.pi / F)
    return (jnp.cos(angles), jnp.sin(angles))


def cross_to_lags(cross_real, cross_imag, tables):
    cos_table, sin_table = tables
    lag_blocks = []
    for block_index in range(LAGS // LAG_BLK):
        turn_cos, turn_sin = lag_turn(block_index)
        rot_real = (cross_real * turn_cos - cross_imag * turn_sin).astype(jnp.bfloat16)
        rot_imag = (cross_real * turn_sin + cross_imag * turn_cos).astype(jnp.bfloat16)
        lag_blocks.append(
            jnp.dot(rot_real, cos_table, preferred_element_type=jnp.float32)
            + jnp.dot(rot_imag, sin_table, preferred_element_type=jnp.float32)
        )
    return jnp.concatenate(lag_blocks, axis=1) * F ** (-0.5)


def outer_cross(left_rows, right_rows):
    left_float = left_rows.astype(jnp.float32)
    right_float = right_rows.astype(jnp.float32)
    segments = left_rows.shape[1]
    cross_real = jnp.zeros((left_rows.shape[0], right_rows.shape[0], F), jnp.float32)
    cross_imag = jnp.zeros((left_rows.shape[0], right_rows.shape[0], F), jnp.float32)
    for segment in range(segments):
        left_real = left_float[:, segment, 0][:, None]
        left_imag = left_float[:, segment, 1][:, None]
        right_real = right_float[:, segment, 0][None]
        right_imag = right_float[:, segment, 1][None]
        cross_real = cross_real + (left_real * right_real + left_imag * right_imag)
        cross_imag = cross_imag + (left_imag * right_real - left_real * right_imag)
    inverse = 1.0 / segments
    return ((cross_real * inverse).reshape(-1, F), (cross_imag * inverse).reshape(-1, F))


def pair_cross(left_rows, right_rows):
    left_float = left_rows.astype(jnp.float32)
    right_float = right_rows.astype(jnp.float32)
    segments = left_rows.shape[1]
    cross_real = jnp.zeros((left_rows.shape[0], F), jnp.float32)
    cross_imag = jnp.zeros((left_rows.shape[0], F), jnp.float32)
    for segment in range(segments):
        left_real = left_float[:, segment, 0]
        left_imag = left_float[:, segment, 1]
        right_real = right_float[:, segment, 0]
        right_imag = right_float[:, segment, 1]
        cross_real = cross_real + (left_real * right_real + left_imag * right_imag)
        cross_imag = cross_imag + (left_imag * right_real - left_real * right_imag)
    inverse = 1.0 / segments
    return (cross_real * inverse, cross_imag * inverse)


def outer_lags(left_rows, right_rows, tables):
    cross_real, cross_imag = outer_cross(left_rows, right_rows)
    return cross_to_lags(cross_real, cross_imag, tables).reshape(
        left_rows.shape[0], right_rows.shape[0], LAGS
    )


def on_device(spectra, source_pick, pair_remote, pair_local, pair_count):
    white = whiten(spectra)
    channels_here = white.shape[0]
    flattened = white.reshape(channels_here, -1)
    tables = lag_tables()
    channel_ids = jnp.arange(channels_here, dtype=jnp.int32)
    picker = (channel_ids[None, :] == source_pick[:, None]).astype(jnp.bfloat16)
    source = jnp.dot(picker, flattened, preferred_element_type=jnp.float32).astype(jnp.bfloat16)
    source = source.reshape((1,) + white.shape[1:])

    def correlate(shard_rows):
        rows_here = shard_rows.shape[0]
        if rows_here > source_block and rows_here % source_block == 0:
            portions = shard_rows.reshape(
                (rows_here // source_block, source_block) + shard_rows.shape[1:]
            )
            result = lax.map(lambda portion: outer_lags(white, portion, tables), portions)
            return jnp.transpose(result, (1, 0, 2, 3)).reshape(channels_here, rows_here, LAGS)
        return outer_lags(white, shard_rows, tables)

    group_corr = correlate(lax.all_gather(source, "dev", axis=0, tiled=True))
    groups = lax.axis_size("grp")
    remote_ids = pair_remote.reshape(groups, -1)
    local_ids = pair_local.reshape(groups, -1)
    slot_count = remote_ids.shape[1]
    gathered = lax.all_gather(white[None], "grp", axis=0, tiled=True)
    remote_picker = (remote_ids[:, :, None] == channel_ids[None, None, :]).astype(jnp.bfloat16)
    remote_rows = jnp.einsum(
        "hkc,hcx->hkx",
        remote_picker,
        gathered.reshape(groups, channels_here, -1),
        preferred_element_type=jnp.float32,
    ).astype(jnp.bfloat16)
    local_picker = (local_ids.reshape(-1)[:, None] == channel_ids[None, :]).astype(jnp.bfloat16)
    local_rows = jnp.dot(local_picker, flattened, preferred_element_type=jnp.float32).astype(
        jnp.bfloat16
    )
    cross_real, cross_imag = pair_cross(
        local_rows.reshape((-1,) + white.shape[1:]), remote_rows.reshape((-1,) + white.shape[1:])
    )
    lags_out = cross_to_lags(cross_real, cross_imag, tables).reshape(groups, slot_count, LAGS)
    valid_mask = (jnp.arange(slot_count)[None, :] < pair_count.reshape(groups, 1)).astype(
        jnp.float32
    )
    cross_corr = (lags_out * valid_mask[:, :, None]).reshape(1, 1, groups, slot_count, LAGS)
    return (group_corr, cross_corr)


def solution(mesh):
    return jax.shard_map(
        on_device,
        mesh=mesh,
        in_specs=(
            P(("grp", "dev"), None, None, None),
            P(("grp", "dev")),
            P("grp", "dev", None, None),
            P("grp", "dev", None, None),
            P("grp", "dev", None),
        ),
        out_specs=(P(("grp", "dev"), None, None), P("grp", "dev", None, None, None)),
        check_vma=False,
    )
```

profile of v0, /device:TPU:0, one launch (start us, length us, event | category | flops | bytes accessed | tf_op | source)
XLA Modules:
  0.0 193.7 jit_solution(853574657091264866)
XLA Ops:
  1.3 0.8 eq.73
  2.0 0.7 compare_select_fusion
  3.0 1.4 copy.52
  5.4 0.3 fusion.152
  6.3 24.6 %all_gather.6 = bf16[16,2,2,4096]{3,2,1,0:T(2,128)(2,1)S(1)} all-gather(bf16[1,2,2,4096]{3,2,1,0:T(2,128)(2,1)S(1)} %reshape.266), channel_id=1, replica_groups=mesh['grp'=2,'dev'=16] {'dev'}, dimensions={0}, use_global_device_ids=true | all-gather | bytes 557056 | tf_op jit(solution)/shard_map/all_gather | solution.py:112
  30.9 9.7 %all-gather = bf16[16,2,2,4096]{3,0,2,1:T(8,128)(2,1)S(1)} all-gather(bf16[8,2,2,4096]{3,0,2,1:T(8,128)(2,1)S(1)} %get-tuple-element.3), channel_id=2, replica_groups=mesh['grp'=2,'dev'=16] {'grp'}, dimensions={0}, use_global_device_ids=true | all-gather | bytes 786432 | tf_op jit(solution)/shard_map/all_gather | solution.py:117
  40.7 0.5 copy.53
  41.2 0.4 reshape.267
  41.6 0.3 fusion
  42.0 0.3 reshape.269
  42.8 9.9 %fusion.25 = f32[4,128]{1,0:T(4,128)S(1)} fusion(f32[4,1,1,4096]{3,0,2,1:T(4,128)S(1)} %get-tuple-element.19, f32[4,1,1,4096]{3,0,2,1:T(4,128)S(1)} %get-tuple-element.18, f32[4096]{0:T(1024)S(1)} %get-tuple-element.38, f32[4096]{0:T(1024)S(1)} %get-tuple-element.39), kind=kOutput, calls=%fused_computation.58 | convolution fusion | flops 12124160 | bytes 165888 | tf_op jit(solution)/shard_map/dot_general | solution.py:45
  52.7 10.0 %convolution_add_fusion.6 = f32[4,128]{1,0:T(4,128)S(1)} fusion(f32[4,128]{1,0:T(4,128)S(1)} %fusion.25, f32[4,1,1,4096]{3,0,2,1:T(4,128)S(1)} %get-tuple-element.19, f32[4,1,1,4096]{3,0,2,1:T(4,128)S(1)} %get-tuple-element.18, f32[4096]{0:T(1024)S(1)} %get-tuple-element.38, f32[4096]{0:T(1024)S(1)} %get-tuple-element.39), kind=kOutput, calls=%fused_computation.54 | convolution fusion | flops 12648960 | bytes 167936 | tf_op jit(solution)/shard_map/dot_general | solution.py:46
  62.7 9.9 %fusion.24 = f32[4,128]{1,0:T(4,128)S(1)} fusion(f32[4,1,1,4096]{3,0,2,1:T(4,128)S(1)} %get-tuple-element.19, f32[4,1,1,4096]{3,0,2,1:T(4,128)S(1)} %get-tuple-element.18), kind=kOutput, calls=%fused_computation.57 | convolution fusion | flops 12124160 | bytes 133120 | tf_op jit(solution)/shard_map/dot_general | solution.py:45
  72.5 10.0 %convolution_add_fusion.5 = f32[4,128]{1,0:T(4,128)S(1)} fusion(f32[4,128]{1,0:T(4,128)S(1)} %fusion.24, f32[4,1,1,4096]{3,0,2,1:T(4,128)S(1)} %get-tuple-element.19, f32[4,1,1,4096]{3,0,2,1:T(4,128)S(1)} %get-tuple-element.18), kind=kOutput, calls=%fused_computation.53 | convolution fusion | flops 12648960 | bytes 135168 | tf_op jit(solution)/shard_map/dot_general | solution.py:46
  82.6 9.9 %fusion.23 = f32[4,128]{1,0:T(4,128)S(1)} fusion(f32[4,1,1,4096]{3,0,2,1:T(4,128)S(1)} %get-tuple-element.19, f32[4,1,1,4096]{3,0,2,1:T(4,128)S(1)} %get-tuple-element.18, f32[4096]{0:T(1024)S(1)} %get-tuple-element.36, f32[4096]{0:T(1024)S(1)} %get-tuple-element.37), kind=kOutput, calls=%fused_computation.56 | convolution fusion | flops 12124160 | bytes 165888 | tf_op jit(solution)/shard_map/dot_general | solution.py:45
  92.4 10.0 %convolution_add_fusion.4 = f32[4,128]{1,0:T(4,128)S(1)} fusion(f32[4,128]{1,0:T(4,128)S(1)} %fusion.23, f32[4,1,1,4096]{3,0,2,1:T(4,128)S(1)} %get-tuple-element.19, f32[4,1,1,4096]{3,0,2,1:T(4,128)S(1)} %get-tuple-element.18, f32[4096]{0:T(1024)S(1)} %get-tuple-element.36, f32[4096]{0:T(1024)S(1)} %get-tuple-element.37), kind=kOutput, calls=%fused_computation.52 | convolution fusion | flops 12648960 | bytes 167936 | tf_op jit(solution)/shard_map/dot_general | solution.py:46
  102.4 9.9 %fusion.26 = f32[4,128]{1,0:T(4,128)S(1)} fusion(f32[4,1,1,4096]{3,0,2,1:T(4,128)S(1)} %get-tuple-element.19, f32[4,1,1,4096]{3,0,2,1:T(4,128)S(1)} %get-tuple-element.18, f32[4096]{0:T(1024)S(1)} %get-tuple-element.40, f32[4096]{0:T(1024)S(1)} %get-tuple-element.41), kind=kOutput, calls=%fused_computation.59 | convolution fusion | flops 12124160 | bytes 165888 | tf_op jit(solution)/shard_map/dot_general | solution.py:45
  112.3 10.0 %convolution_add_fusion.7 = f32[4,128]{1,0:T(4,128)S(1)} fusion(f32[4,128]{1,0:T(4,128)S(1)} %fusion.26, f32[4,1,1,4096]{3,0,2,1:T(4,128)S(1)} %get-tuple-element.19, f32[4,1,1,4096]{3,0,2,1:T(4,128)S(1)} %get-tuple-element.18, f32[4096]{0:T(1024)S(1)} %get-tuple-element.40, f32[4096]{0:T(1024)S(1)} %get-tuple-element.41), kind=kOutput, calls=%fused_computation.55 | convolution fusion | flops 12648960 | bytes 167936 | tf_op jit(solution)/shard_map/dot_general | solution.py:46
  122.3 0.7 maximum_multiply_fusion.1
  123.0 1.2 fusion.153
  124.5 0.3 copy_bitcast_fusion
  124.8 1.0 add_add_fusion
  125.8 2.6 %fusion.7 = (bf16[128,4096]{1,0:T(8,128)(2,1)S(1)}, bf16[128,4096]{1,0:T(8,128)(2,1)S(1)}, bf16[128,4096]{1,0:T(8,128)(2,1)S(1)}, bf16[128,4096]{1,0:T(8,128)(2,...) fusion(f32[8,16,4096]{2,1,0:T(8,128)S(1)} %get-tuple-element.17, ...), kind=kLoop, calls=%fused_computation.20 | loop fusion | flops 16777216 | bytes 12681216 | tf_op jit(solution)/shard_map/convert_element_type | solution.py:43
  128.3 7.8 %fusion.30 = f32[128,128]{1,0:T(8,128)S(1)} fusion(bf16[128,4096]{1,0:T(8,128)(2,1)S(1)} %get-tuple-element.5), kind=kOutput, calls=%fused_computation.63 | convolution fusion | flops 142082048 | bytes 1114112 | tf_op jit(solution)/shard_map/dot_general | solution.py:45
  136.2 8.2 %convolution_add_fusion.3 = f32[128,128]{1,0:T(8,128)S(1)} fusion(f32[128,128]{1,0:T(8,128)S(1)} %fusion.30, bf16[128,4096]{1,0:T(8,128)(2,1)S(1)} %get-tuple-element.4), kind=kOutput, calls=%fused_computation.51 | convolution fusion | flops 142622720 | bytes 1179648 | tf_op jit(solution)/shard_map/dot_general | solution.py:46
  144.3 8.2 %fusion.29 = f32[128,128]{1,0:T(8,128)S(1)} fusion(bf16[128,4096]{1,0:T(8,128)(2,1)S(1)} %get-tuple-element.10), kind=kOutput, calls=%fused_computation.62 | convolution fusion | flops 142082048 | bytes 1114112 | tf_op jit(solution)/shard_map/dot_general | solution.py:45
  152.6 8.0 %convolution_add_fusion.2 = f32[128,128]{1,0:T(8,128)S(1)} fusion(f32[128,128]{1,0:T(8,128)S(1)} %fusion.29, bf16[128,4096]{1,0:T(8,128)(2,1)S(1)} %get-tuple-element.11), kind=kOutput, calls=%fused_computation.50 | convolution fusion | flops 142622720 | bytes 1179648 | tf_op jit(solution)/shard_map/dot_general | solution.py:46
  160.5 8.0 %fusion.28 = f32[128,128]{1,0:T(8,128)S(1)} fusion(bf16[128,4096]{1,0:T(8,128)(2,1)S(1)} %get-tuple-element.12), kind=kOutput, calls=%fused_computation.61 | convolution fusion | flops 142082048 | bytes 1114112 | tf_op jit(solution)/shard_map/dot_general | solution.py:45
  168.5 8.2 %convolution_add_fusion.1 = f32[128,128]{1,0:T(8,128)S(1)} fusion(f32[128,128]{1,0:T(8,128)S(1)} %fusion.28, bf16[128,4096]{1,0:T(8,128)(2,1)S(1)} %get-tuple-element.13), kind=kOutput, calls=%fused_computation.49 | convolution fusion | flops 142622720 | bytes 1179648 | tf_op jit(solution)/shard_map/dot_general | solution.py:46
  176.7 7.8 %fusion.27 = f32[128,128]{1,0:T(8,128)S(1)} fusion(bf16[128,4096]{1,0:T(8,128)(2,1)S(1)} %get-tuple-element.14), kind=kOutput, calls=%fused_computation.60 | convolution fusion | flops 142082048 | bytes 1114112 | tf_op jit(solution)/shard_map/dot_general | solution.py:45
  184.5 8.2 %convolution_add_fusion = f32[128,128]{1,0:T(8,128)S(1)} fusion(f32[128,128]{1,0:T(8,128)S(1)} %fusion.27, bf16[128,4096]{1,0:T(8,128)(2,1)S(1)} %get-tuple-element.15), kind=kOutput, calls=%fused_computation.48 | convolution fusion | flops 142622720 | bytes 1179648 | tf_op jit(solution)/shard_map/dot_general | solution.py:46
  192.8 0.7 maximum_multiply_fusion
  (22 shorter events, 2.5 us)
Async XLA Ops:
  3.0 2.4 %copy-start = (f32[8,2,2,4096]{3,2,1,0:T(2,128)S(1)}, f32[8,2,2,4096]{3,2,1,0:T(2,128)}, u32[]{:S(2)}) copy-start(f32[8,2,2,4096]{3,2,1,0:T(2,128)} %param.5) | copy-start | bytes 1572868
  6.0 35.6 %copy-start.1 = (s32[1,1,2,2]{3,2,1,0:T(2,128)S(1)}, s32[1,1,2,2]{3,2,1,0:T(2,128)}, u32[]{:S(2)}) copy-start(s32[1,1,2,2]{3,2,1,0:T(2,128)} %param.7) | copy-start | bytes 52
where the time goes:
time: 196 us; the launch traced here: 194 us
  matrix products  145 us (74%)
  blocking collectives  34.3 us (17%)
  other arithmetic  6.76 us (3%)
  local copies, waits for them, and re-layouts  6.14 us (3%)
    dot_general x8, matrix products, cross_to_lags(): jnp.dot(rot_imag, sin_table, preferred_element_type=jnp.float32)  72.5 us
    dot_general x8, matrix products, cross_to_lags(): jnp.dot(rot_real, cos_table, preferred_element_type=jnp.float32)  71.3 us
    all_gather x1, blocking collectives, on_device(): group_corr = correlate(lax.all_gather(source, 'dev', axis=0, tiled=True))  24.6 us
    all_gather x1, blocking collectives, on_device(): gathered = lax.all_gather(white[None], 'grp', axis=0, tiled=True)  9.75 us

commit v1 on v0

--- a/solution.py
+++ b/solution.py
@@ -9,6 +9,28 @@
 LAG_BLK = 128
 BAND = 64
 source_block = 16
+
+
+def in_order(blocks, dim):
+    blocks = jnp.moveaxis(blocks, 0, dim)
+    shape = blocks.shape
+    return blocks.reshape(*shape[:dim], shape[dim] * shape[dim + 1], *shape[dim + 2 :])
+
+
+def collected_by_bits(x, axis):
+    count = lax.axis_size(axis)
+    blocks = x[None]
+    for level in range(count.bit_length() - 1):
+        apart = 1 << level
+        other = lax.ppermute(blocks, axis, [(i, i ^ apart) for i in range(count)])
+        both = jnp.stack([blocks, other])
+        upper = lax.axis_index(axis) >> level & 1
+        blocks = jnp.where(upper == 0, both, both[::-1]).reshape(-1, *x.shape)
+    return blocks
+
+
+def doubled_up(array, axis, dim):
+    return in_order(collected_by_bits(array, axis), dim)
 
 
 def whiten(spectra):
@@ -109,7 +131,7 @@
             return jnp.transpose(result, (1, 0, 2, 3)).reshape(channels_here, rows_here, LAGS)
         return outer_lags(white, shard_rows, tables)
 
-    group_corr = correlate(lax.all_gather(source, "dev", axis=0, tiled=True))
+    group_corr = correlate(doubled_up(source, "dev", 0))
     groups = lax.axis_size("grp")
     remote_ids = pair_remote.reshape(groups, -1)
     local_ids = pair_local.reshape(groups, -1)

time: 196 us -> 192 us (0.980)
  blocking collectives: 34.3 us -> 10.2 us
  waiting for transfers between devices: 0 us -> 10.4 us
  starting transfers between devices: 0 us -> 6.6 us
  other arithmetic: 6.76 us -> 8.93 us
    all_gather x1 -> x0, blocking collectives: 24.6 us -> none  [on_device(): group_corr = correlate(lax.all_gather(source, 'dev', axis=0, tiled=True))]
    ppermute x0 -> x4, waiting for transfers between devices: none -> 10.4 us  [collected_by_bits(): other = lax.ppermute(blocks, axis, [(i, i ^ apart) for i in range(count)])]
    ppermute x0 -> x4, starting transfers between devices: none -> 6.6 us  [collected_by_bits(): other = lax.ppermute(blocks, axis, [(i, i ^ apart) for i in range(count)])]
  transfers between devices with their start and end apart: 0 -> 4, of which waited for: 0 -> 1; matrix products, arithmetic and copies ran while one was open for 0% -> 44% of each run, Pallas kernels for 0% -> 0%
where the time goes in v1:
time: 192 us; the launch traced here: 189 us
  matrix products  145 us (76%)
  waiting for transfers between devices  10.4 us (5%)
  blocking collectives  10.2 us (5%)
  other arithmetic  8.93 us (5%)
  starting transfers between devices  6.6 us (3%)
  local copies, waits for them, and re-layouts  5.44 us (3%)
    dot_general x8, matrix products, cross_to_lags(): jnp.dot(rot_imag, sin_table, preferred_element_type=jnp.float32)  72.5 us
    dot_general x8, matrix products, cross_to_lags(): jnp.dot(rot_real, cos_table, preferred_element_type=jnp.float32)  71.9 us
    ppermute x4, waiting for transfers between devices, collected_by_bits(): other = lax.ppermute(blocks, axis, [(i, i ^ apart) for i in range(count)])  10.4 us
    all_gather x1, blocking collectives, on_device(): gathered = lax.all_gather(white[None], 'grp', axis=0, tiled=True)  10.2 us
    ppermute x4, starting transfers between devices, collected_by_bits(): other = lax.ppermute(blocks, axis, [(i, i ^ apart) for i in range(count)])  6.6 us
  transfers between devices with their start and end apart: 4, of which 1 were waited for; matrix products, arithmetic and copies ran while one was open for 44% of the time, Pallas kernels for 0%

profile of v1, /device:TPU:0, one launch (start us, length us, event | category | flops | bytes accessed | tf_op | source)
XLA Modules:
  0.0 188.7 jit_solution(4348212725715246316)
XLA Ops:
  1.3 1.4 copy.39
  4.2 0.5 collective-permute-start
  5.0 10.2 %all-gather = bf16[16,2,2,4096]{3,0,2,1:T(8,128)(2,1)S(1)} all-gather(bf16[8,2,2,4096]{3,0,2,1:T(8,128)(2,1)S(1)} %get-tuple-element.3), channel_id=2, replica_groups=mesh['grp'=2,'dev'=16] {'grp'}, dimensions={0}, use_global_device_ids=true | all-gather | bytes 786432 | tf_op jit(solution)/shard_map/all_gather | solution.py:139
  15.6 0.5 copy.40
  17.7 10.4 %fusion.25 = f32[4,128]{1,0:T(4,128)S(1)} fusion(f32[4,1,1,4096]{3,0,2,1:T(4,128)S(1)} %get-tuple-element.23, f32[4,1,1,4096]{3,0,2,1:T(4,128)S(1)} %get-tuple-element.22, f32[4096]{0:T(1024)S(1)} %get-tuple-element.40, f32[4096]{0:T(1024)S(1)} %get-tuple-element.41), kind=kOutput, calls=%fused_computation.58 | convolution fusion | flops 12124160 | bytes 165888 | tf_op jit(solution)/shard_map/dot_general | solution.py:67
  28.1 10.0 %convolution_add_fusion.6 = f32[4,128]{1,0:T(4,128)S(1)} fusion(f32[4,128]{1,0:T(4,128)S(1)} %fusion.25, f32[4,1,1,4096]{3,0,2,1:T(4,128)S(1)} %get-tuple-element.23, f32[4,1,1,4096]{3,0,2,1:T(4,128)S(1)} %get-tuple-element.22, f32[4096]{0:T(1024)S(1)} %get-tuple-element.40, f32[4096]{0:T(1024)S(1)} %get-tuple-element.41), kind=kOutput, calls=%fused_computation.54 | convolution fusion | flops 12648960 | bytes 167936 | tf_op jit(solution)/shard_map/dot_general | solution.py:68
  38.1 9.9 %fusion.23 = f32[4,128]{1,0:T(4,128)S(1)} fusion(f32[4,1,1,4096]{3,0,2,1:T(4,128)S(1)} %get-tuple-element.23, f32[4,1,1,4096]{3,0,2,1:T(4,128)S(1)} %get-tuple-element.22, f32[4096]{0:T(1024)S(1)} %get-tuple-element.38, f32[4096]{0:T(1024)S(1)} %get-tuple-element.39), kind=kOutput, calls=%fused_computation.56 | convolution fusion | flops 12124160 | bytes 165888 | tf_op jit(solution)/shard_map/dot_general | solution.py:67
  48.0 10.0 %convolution_add_fusion.4 = f32[4,128]{1,0:T(4,128)S(1)} fusion(f32[4,128]{1,0:T(4,128)S(1)} %fusion.23, f32[4,1,1,4096]{3,0,2,1:T(4,128)S(1)} %get-tuple-element.23, f32[4,1,1,4096]{3,0,2,1:T(4,128)S(1)} %get-tuple-element.22, f32[4096]{0:T(1024)S(1)} %get-tuple-element.38, f32[4096]{0:T(1024)S(1)} %get-tuple-element.39), kind=kOutput, calls=%fused_computation.52 | convolution fusion | flops 12648960 | bytes 167936 | tf_op jit(solution)/shard_map/dot_general | solution.py:68
  58.0 9.9 %fusion.26 = f32[4,128]{1,0:T(4,128)S(1)} fusion(f32[4,1,1,4096]{3,0,2,1:T(4,128)S(1)} %get-tuple-element.23, f32[4,1,1,4096]{3,0,2,1:T(4,128)S(1)} %get-tuple-element.22, f32[4096]{0:T(1024)S(1)} %get-tuple-element.42, f32[4096]{0:T(1024)S(1)} %get-tuple-element.43), kind=kOutput, calls=%fused_computation.59 | convolution fusion | flops 12124160 | bytes 165888 | tf_op jit(solution)/shard_map/dot_general | solution.py:67
  67.9 10.0 %convolution_add_fusion.7 = f32[4,128]{1,0:T(4,128)S(1)} fusion(f32[4,128]{1,0:T(4,128)S(1)} %fusion.26, f32[4,1,1,4096]{3,0,2,1:T(4,128)S(1)} %get-tuple-element.23, f32[4,1,1,4096]{3,0,2,1:T(4,128)S(1)} %get-tuple-element.22, f32[4096]{0:T(1024)S(1)} %get-tuple-element.42, f32[4096]{0:T(1024)S(1)} %get-tuple-element.43), kind=kOutput, calls=%fused_computation.55 | convolution fusion | flops 12648960 | bytes 167936 | tf_op jit(solution)/shard_map/dot_general | solution.py:68
  78.1 1.8 collective-permute-start.1
  79.9 9.8 %fusion.24 = f32[4,128]{1,0:T(4,128)S(1)} fusion(f32[4,1,1,4096]{3,0,2,1:T(4,128)S(1)} %get-tuple-element.23, f32[4,1,1,4096]{3,0,2,1:T(4,128)S(1)} %get-tuple-element.22), kind=kOutput, calls=%fused_computation.57 | convolution fusion | flops 12124160 | bytes 133120 | tf_op jit(solution)/shard_map/dot_general | solution.py:67
  90.1 1.6 collective-permute-start.2
  91.7 10.0 %convolution_add_fusion.5 = f32[4,128]{1,0:T(4,128)S(1)} fusion(f32[4,128]{1,0:T(4,128)S(1)} %fusion.24, f32[4,1,1,4096]{3,0,2,1:T(4,128)S(1)} %get-tuple-element.23, f32[4,1,1,4096]{3,0,2,1:T(4,128)S(1)} %get-tuple-element.22), kind=kOutput, calls=%fused_computation.53 | convolution fusion | flops 12648960 | bytes 135168 | tf_op jit(solution)/shard_map/dot_general | solution.py:68
  102.3 2.7 %collective-permute-start.3 = (bf16[8,1,2,2,4096]{4,3,2,0,1:T(2,128)(2,1)S(1)}, bf16[8,1,2,2,4096]{4,3,2,0,1:T(2,128)(2,1)S(1)}, u32[]{:S(2)}, u32[]{:S(2)}) collective-permute-start(bf16[8,1,2,2,4096]{4,3,2,0,1:T(2,128)(2,1)S(1)} %bitcast.220), channel_id=1, source_target_pairs={{0,8},{1,9},{2,10},{3,11},{4,12},{5,13},{6,14},{7,15},{8,0},{9,1},... | collective-permute-start | bytes 786440 | tf_op jit(solution)/shard_map/ppermute | solution.py:25
  105.1 0.7 maximum_multiply_fusion.1
  105.7 10.4 %collective-permute-done.3 = bf16[8,1,2,2,4096]{4,3,2,0,1:T(2,128)(2,1)S(1)} collective-permute-done((bf16[8,1,2,2,4096]{4,3,2,0,1:T(2,128)(2,1)S(1)}, bf16[8,1,2,2,4096]{4,3,2,0,1:T(2,128)(2,1)S(1)}, u32[]{:S(2)}, u32[]{:S(2)}) %collective-permute-start.3) | collective-permute-done | bytes 262176 | tf_op jit(solution)/shard_map/ppermute | solution.py:25
  116.2 0.7 pad_maximum_fusion
  116.9 0.5 broadcast_select_fusion
  117.5 0.5 bitcast_convert_fusion
  117.9 1.1 fusion.155
  119.7 1.0 add_add_fusion
  120.7 2.6 %fusion.7 = (bf16[128,4096]{1,0:T(8,128)(2,1)S(1)}, bf16[128,4096]{1,0:T(8,128)(2,1)S(1)}, bf16[128,4096]{1,0:T(8,128)(2,1)S(1)}, bf16[128,4096]{1,0:T(8,128)(2,...) fusion(f32[8,16,4096]{2,1,0:T(8,128)S(1)} %get-tuple-element.17, ...), kind=kLoop, calls=%fused_computation.20 | loop fusion | flops 16777216 | bytes 12681216 | tf_op jit(solution)/shard_map/convert_element_type | solution.py:65
  123.2 7.8 %fusion.30 = f32[128,128]{1,0:T(8,128)S(1)} fusion(bf16[128,4096]{1,0:T(8,128)(2,1)S(1)} %get-tuple-element.5), kind=kOutput, calls=%fused_computation.63 | convolution fusion | flops 142082048 | bytes 1114112 | tf_op jit(solution)/shard_map/dot_general | solution.py:67
  131.1 8.0 %fusion.29 = f32[128,128]{1,0:T(8,128)S(1)} fusion(bf16[128,4096]{1,0:T(8,128)(2,1)S(1)} %get-tuple-element.10), kind=kOutput, calls=%fused_computation.62 | convolution fusion | flops 142082048 | bytes 1114112 | tf_op jit(solution)/shard_map/dot_general | solution.py:67
  139.1 8.2 %fusion.28 = f32[128,128]{1,0:T(8,128)S(1)} fusion(bf16[128,4096]{1,0:T(8,128)(2,1)S(1)} %get-tuple-element.12), kind=kOutput, calls=%fused_computation.61 | convolution fusion | flops 142082048 | bytes 1114112 | tf_op jit(solution)/shard_map/dot_general | solution.py:67
  147.3 7.8 %fusion.27 = f32[128,128]{1,0:T(8,128)S(1)} fusion(bf16[128,4096]{1,0:T(8,128)(2,1)S(1)} %get-tuple-element.14), kind=kOutput, calls=%fused_computation.60 | convolution fusion | flops 142082048 | bytes 1114112 | tf_op jit(solution)/shard_map/dot_general | solution.py:67
  155.2 8.1 %convolution_add_fusion.3 = f32[128,128]{1,0:T(8,128)S(1)} fusion(f32[128,128]{1,0:T(8,128)S(1)} %fusion.30, bf16[128,4096]{1,0:T(8,128)(2,1)S(1)} %get-tuple-element.4), kind=kOutput, calls=%fused_computation.51 | convolution fusion | flops 142622720 | bytes 1179648 | tf_op jit(solution)/shard_map/dot_general | solution.py:68
  163.3 8.2 %convolution_add_fusion.2 = f32[128,128]{1,0:T(8,128)S(1)} fusion(f32[128,128]{1,0:T(8,128)S(1)} %fusion.29, bf16[128,4096]{1,0:T(8,128)(2,1)S(1)} %get-tuple-element.11), kind=kOutput, calls=%fused_computation.50 | convolution fusion | flops 142622720 | bytes 1179648 | tf_op jit(solution)/shard_map/dot_general | solution.py:68
  171.5 8.0 %convolution_add_fusion.1 = f32[128,128]{1,0:T(8,128)S(1)} fusion(f32[128,128]{1,0:T(8,128)S(1)} %fusion.28, bf16[128,4096]{1,0:T(8,128)(2,1)S(1)} %get-tuple-element.13), kind=kOutput, calls=%fused_computation.49 | convolution fusion | flops 142622720 | bytes 1179648 | tf_op jit(solution)/shard_map/dot_general | solution.py:68
  179.4 8.2 %convolution_add_fusion = f32[128,128]{1,0:T(8,128)S(1)} fusion(f32[128,128]{1,0:T(8,128)S(1)} %fusion.27, bf16[128,4096]{1,0:T(8,128)(2,1)S(1)} %get-tuple-element.15), kind=kOutput, calls=%fused_computation.48 | convolution fusion | flops 142622720 | bytes 1179648 | tf_op jit(solution)/shard_map/dot_general | solution.py:68
  187.7 0.7 maximum_multiply_fusion
  (43 shorter events, 5.5 us)
Async XLA Ops:
  1.3 2.4 %copy-start = (f32[8,2,2,4096]{3,2,1,0:T(2,128)S(1)}, f32[8,2,2,4096]{3,2,1,0:T(2,128)}, u32[]{:S(2)}) copy-start(f32[8,2,2,4096]{3,2,1,0:T(2,128)} %param.5) | copy-start | bytes 1572868
  3.2 11.9 %copy-start.2 = (s32[1,1,2,2]{3,2,1,0:T(2,128)S(1)}, s32[1,1,2,2]{3,2,1,0:T(2,128)}, u32[]{:S(2)}) copy-start(s32[1,1,2,2]{3,2,1,0:T(2,128)} %param.8) | copy-start | bytes 52
  4.2 73.7 %collective-permute-start = (bf16[1,1,2,2,4096]{4,3,2,1,0:T(2,128)(2,1)S(1)}, bf16[1,1,2,2,4096]{4,3,2,1,0:T(2,128)(2,1)S(1)}, u32[]{:S(2)}, u32[]{:S(2)}) collective-permute-start(bf16[1,1,2,2,4096]{4,3,2,1,0:T(2,128)(2,1)S(1)} %broadcast_in_dim_reshape.2), channel_id=1, source_target_pairs={{0,1},{1,0},{2,3},{3,2},{4,5},{5,4},{6,7},{7,6},{8,9},{9,8},{10,11... | collective-permute-start | bytes 98312 | tf_op jit(solution)/shard_map/ppermute | solution.py:25
  15.2 1.4 copy-start.1
  78.1 11.6 %collective-permute-start.1 = (bf16[2,1,2,2,4096]{4,3,2,0,1:T(2,128)(2,1)S(1)}, bf16[2,1,2,2,4096]{4,3,2,0,1:T(2,128)(2,1)S(1)}, u32[]{:S(2)}, u32[]{:S(2)}) collective-permute-start(bf16[2,1,2,2,4096]{4,3,2,0,1:T(2,128)(2,1)S(1)} %get-tuple-element.33), channel_id=1, source_target_pairs={{0,2},{1,3},{2,0},{3,1},{4,6},{5,7},{6,4},{7,5},{8,10},{9,11},{10,... | collective-permute-start | bytes 196616 | tf_op jit(solution)/shard_map/ppermute | solution.py:25
  90.0 14.9 %copy-start.3 = (s32[1,1,2]{2,1,0:T(1,128)S(1)}, s32[1,1,2]{2,1,0:T(1,128)}, u32[]{:S(2)}) copy-start(s32[1,1,2]{2,1,0:T(1,128)} %param.9) | copy-start | bytes 28
  90.1 11.6 %collective-permute-start.2 = (bf16[4,1,2,2,4096]{4,3,2,0,1:T(2,128)(2,1)S(1)}, bf16[4,1,2,2,4096]{4,3,2,0,1:T(2,128)(2,1)S(1)}, u32[]{:S(2)}, u32[]{:S(2)}) collective-permute-start(bf16[4,1,2,2,4096]{4,3,2,0,1:T(2,128)(2,1)S(1)} %bitcast.223), channel_id=1, source_target_pairs={{0,4},{1,5},{2,6},{3,7},{4,0},{5,1},{6,2},{7,3},{8,12},{9,13},{10,... | collective-permute-start | bytes 393224 | tf_op jit(solution)/shard_map/ppermute | solution.py:25
  102.3 13.8 %collective-permute-start.3 = (bf16[8,1,2,2,4096]{4,3,2,0,1:T(2,128)(2,1)S(1)}, bf16[8,1,2,2,4096]{4,3,2,0,1:T(2,128)(2,1)S(1)}, u32[]{:S(2)}, u32[]{:S(2)}) collective-permute-start(bf16[8,1,2,2,4096]{4,3,2,0,1:T(2,128)(2,1)S(1)} %bitcast.220), channel_id=1, source_target_pairs={{0,8},{1,9},{2,10},{3,11},{4,12},{5,13},{6,14},{7,15},{8,0},{9,1},... | collective-permute-start | bytes 786440 | tf_op jit(solution)/shard_map/ppermute | solution.py:25
